TPU v7x, 32 devices: a whole 2x2x4 slice. The times are simulated.
32 devices in a mesh: dp: 8 (over z, y), head: 4 (over x, core).
Axes of the slice: x: 2, y: 2, z: 4, core: 2. Of those that a mesh axis runs over, the one named last changes fastest.
Arguments:
- tokens: bfloat16 [32768, 512], P(('dp', 'head')), may hold values from -6 to 6
- segments: int32 [32768], P('dp'), may hold values from 0 to 255, never falling along the last dimension, each value on 1 to 256 neighbouring positions
- out_grad: bfloat16 [32768, 512], P(('dp', 'head')), may hold values from -6 to 6
- norm_params: float32 [4, 512], replicated, may hold values from -0.6 to 1.3
- norm_first: float32 [4, 512], replicated, may hold values from -0.0024414062 to 0.0024414062
- norm_second: float32 [4, 512], replicated, may hold values from 7.947286e-08 to 1.2715658e-06
- qkv_weight: float32 [512, 1536], P(None, 'head'), may hold values from -0.25 to 0.25
- qkv_moment: float32 [512, 1536], P(None, 'head'), may hold values from -0.0078125 to 0.0078125
- out_weight: float32 [512, 512], P('head'), may hold values from -2 to 2
- out_moment: float32 [512, 512], P('head'), may hold values from -0.0078125 to 0.0078125
- up_weight: float32 [512, 2048], P(None, ('dp', 'head')), may hold values from -0.25 to 0.25
- up_moment: float32 [512, 2048], P(None, ('dp', 'head')), may hold values from -0.0078125 to 0.0078125
- down_weight: float32 [512, 2048], P(None, ('dp', 'head')), may hold values from -0.125 to 0.125
- down_moment: float32 [512, 2048], P(None, ('dp', 'head')), may hold values from -0.0078125 to 0.0078125
Outputs:
- layer_out: bfloat16 [32768, 512], P(('dp', 'head'))
- input_grad: float32 [32768, 512], P(('dp', 'head'))
- grad_norm: float32 [], replicated
- clipped_grads: float32 [4, 512], replicated
- new_norm_first: float32 [4, 512], replicated
- new_norm_second: float32 [4, 512], replicated
- new_qkv_weight: float32 [512, 1536], P(None, 'head')
- new_qkv_moment: float32 [512, 1536], P(None, 'head')
- new_out_weight: float32 [512, 512], P('head')
- new_out_moment: float32 [512, 512], P('head')
- new_up_weight: float32 [512, 2048], P(None, ('dp', 'head'))
- new_up_moment: float32 [512, 2048], P(None, ('dp', 'head'))
- new_down_weight: float32 [512, 2048], P(None, ('dp', 'head'))
- new_down_moment: float32 [512, 2048], P(None, ('dp', 'head'))
Inputs may be any that keep to these rules, and one draw needn't show every extreme that they name: `segments`: segment ids never fall along the rows; each id covers 1 to 256 consecutive rows.
All inputs are finite; a program needn't handle non-finite values.
Results may differ from a plain program's by a relative error of at most 0.028.
Values may be sent and summed in bfloat16 or wider, within the bound.
A program may use at most 128 MiB of HBM per device.

v0:
```python
import math
import jax
import jax.numpy as jnp
from jax import lax
from jax.sharding import PartitionSpec as P

HEAD_DIM = 64
FF = 2048
SEQ = 512
NS_STEPS = 5
neg_fill = -1000000000.0
norm_eps = 1e-05
ns_a = 3.4445
ns_b = -4.775
ns_c = 2.0315
momentum_decay = 0.95
muon_rate = 0.5
muon_decay = 0.01
beta_one = 0.9
beta_two = 0.95


def normalize(values, gain, shift):
    mean = jnp.mean(values, axis=-1, keepdims=True)
    centered = values - mean
    factor = lax.rsqrt(jnp.mean(centered * centered, axis=-1, keepdims=True) + norm_eps)
    plain = centered * factor
    return (plain * gain + shift, plain, factor)


def normalize_back(upper, plain, factor, gain):
    inner = upper * gain
    lower = factor * (
        inner
        - jnp.mean(inner, axis=-1, keepdims=True)
        - plain * jnp.mean(inner * plain, axis=-1, keepdims=True)
    )
    return (lower, jnp.sum(upper * plain, axis=0), jnp.sum(upper, axis=0))


def masked_scores(query, keys, segment):
    scores = jnp.einsum(
        "qhd,khd->hqk", query, keys, preferred_element_type=jnp.float32
    ) * HEAD_DIM ** (-0.5)
    same = segment[:, None] == segment[None, :]
    return jnp.where(same[None], scores, neg_fill)


def attend_forward(block):
    query, keys, values, segment = block
    scores = masked_scores(query, keys, segment)
    top = jnp.max(scores, axis=-1, keepdims=True)
    weights = jnp.exp(scores - top)
    total = jnp.sum(weights, axis=-1, keepdims=True)
    probs = (weights / total).astype(jnp.bfloat16)
    context = jnp.einsum("hqk,khd->qhd", probs, values, preferred_element_type=jnp.float32)
    return (context.astype(jnp.bfloat16), top + jnp.log(total))


def attend_backward(block):
    query, keys, values, segment, context_grad, lse = block
    scores = masked_scores(query, keys, segment)
    probs = jnp.exp(scores - lse)
    probs_low = probs.astype(jnp.bfloat16)
    probs_grad = jnp.einsum(
        "qhd,khd->hqk", context_grad, values, preferred_element_type=jnp.float32
    )
    inner = jnp.sum(probs * probs_grad, axis=-1, keepdims=True)
    score_grad = (probs * (probs_grad - inner)).astype(jnp.bfloat16)
    query_grad = jnp.einsum(
        "hqk,khd->qhd", score_grad, keys, preferred_element_type=jnp.float32
    ) * HEAD_DIM ** (-0.5)
    key_grad = jnp.einsum(
        "hqk,qhd->khd", score_grad, query, preferred_element_type=jnp.float32
    ) * HEAD_DIM ** (-0.5)
    value_grad = jnp.einsum(
        "hqk,qhd->khd", probs_low, context_grad, preferred_element_type=jnp.float32
    )
    return jnp.stack([query_grad, key_grad, value_grad], axis=2).astype(jnp.bfloat16)


def gram_left(block):
    return lax.dot_general(
        block, block, (((1,), (1,)), ((), ())), preferred_element_type=jnp.float32
    )


def gram_right(block):
    return lax.dot_general(
        block, block, (((0,), (0,)), ((), ())), preferred_element_type=jnp.float32
    )


def squares_of(moment, grad, weight):
    return (
        jnp.stack([jnp.sum(moment * moment), jnp.sum(moment * grad), jnp.sum(grad * grad)]) * weight
    )


def shards(
    tokens,
    segments,
    out_grad,
    norm_params,
    norm_first,
    norm_second,
    qkv_weight,
    qkv_moment,
    out_weight,
    out_moment,
    up_weight,
    up_moment,
    down_weight,
    down_moment,
):
    width = tokens.shape[1]
    group = segments.shape[0]
    narrow = out_weight.shape[0]
    heads_here = narrow // HEAD_DIM
    sequences = group // SEQ
    inputs = tokens.astype(jnp.float32)
    first, first_plain, first_factor = normalize(inputs, norm_params[0], norm_params[1])
    first_all = lax.all_gather(first.astype(jnp.bfloat16), "head", axis=0, tiled=True)
    qkv_low = qkv_weight.astype(jnp.bfloat16)
    out_low = out_weight.astype(jnp.bfloat16)
    mixed = jnp.dot(first_all, qkv_low, preferred_element_type=jnp.float32).astype(jnp.bfloat16)
    mixed = mixed.reshape(sequences, SEQ, heads_here, 3, HEAD_DIM)
    segment_rows = segments.reshape(sequences, SEQ)
    query = mixed[:, :, :, 0]
    keys = mixed[:, :, :, 1]
    values = mixed[:, :, :, 2]
    context, lse = lax.map(attend_forward, (query, keys, values, segment_rows))
    context = context.reshape(group, narrow)
    context_rows = lax.all_to_all(context, "head", split_axis=0, concat_axis=1, tiled=True)
    out_full = lax.all_gather(out_low, "head", axis=0, tiled=True)
    attended = jnp.dot(context_rows, out_full, preferred_element_type=jnp.float32)
    middle = inputs + attended
    second, second_plain, second_factor = normalize(middle, norm_params[2], norm_params[3])
    second_low = second.astype(jnp.bfloat16)
    up_all, down_all = (
        lax.all_gather(up_weight.astype(jnp.bfloat16), ("dp", "head"), axis=1, tiled=True),
        lax.all_gather(down_weight.astype(jnp.bfloat16), ("dp", "head"), axis=1, tiled=True),
    )
    hidden = jnp.dot(second_low, up_all, preferred_element_type=jnp.float32)
    switch = jax.nn.sigmoid(1.702 * hidden)
    active = (hidden * switch).astype(jnp.bfloat16)
    result = middle + lax.dot_general(
        active, down_all, (((1,), (1,)), ((), ())), preferred_element_type=jnp.float32
    )
    layer_out = result.astype(jnp.bfloat16)
    down_grad = lax.dot_general(
        out_grad, active, (((0,), (0,)), ((), ())), preferred_element_type=jnp.float32
    )
    active_grad = jnp.dot(out_grad, down_all, preferred_element_type=jnp.float32)
    hidden_grad = (active_grad * (switch + 1.702 * hidden * switch * (1.0 - switch))).astype(
        jnp.bfloat16
    )
    up_grad = lax.dot_general(
        second_low, hidden_grad, (((0,), (0,)), ((), ())), preferred_element_type=jnp.float32
    )
    second_grad = lax.dot_general(
        hidden_grad, up_all, (((1,), (1,)), ((), ())), preferred_element_type=jnp.float32
    )
    up_part, down_part = (
        lax.psum_scatter(up_grad, ("dp", "head"), scatter_dimension=1, tiled=True),
        lax.psum_scatter(down_grad, ("dp", "head"), scatter_dimension=1, tiled=True),
    )
    middle_lower, gain_two, shift_two = normalize_back(
        second_grad, second_plain, second_factor, norm_params[2]
    )
    middle_grad = out_grad.astype(jnp.float32) + middle_lower
    attended_low = middle_grad.astype(jnp.bfloat16)
    rows_grad = lax.dot_general(
        attended_low, out_full, (((1,), (1,)), ((), ())), preferred_element_type=jnp.float32
    ).astype(jnp.bfloat16)
    context_grad = lax.all_to_all(rows_grad, "head", split_axis=1, concat_axis=0, tiled=True)
    whole_out = lax.dot_general(
        context_rows, attended_low, (((0,), (0,)), ((), ())), preferred_element_type=jnp.float32
    )
    out_part = lax.psum_scatter(
        whole_out.astype(jnp.bfloat16), "head", scatter_dimension=0, tiled=True
    )
    context_grad = context_grad.reshape(sequences, SEQ, heads_here, HEAD_DIM)
    mixed_grad = lax.map(attend_backward, (query, keys, values, segment_rows, context_grad, lse))
    mixed_grad = mixed_grad.reshape(group, 3 * narrow)
    qkv_part = lax.dot_general(
        first_all, mixed_grad, (((0,), (0,)), ((), ())), preferred_element_type=jnp.float32
    )
    mixed_rows = lax.all_to_all(mixed_grad, "head", split_axis=0, concat_axis=1, tiled=True)
    qkv_full = lax.all_gather(qkv_low, "head", axis=1, tiled=True)
    first_grad = lax.dot_general(
        mixed_rows, qkv_full, (((1,), (1,)), ((), ())), preferred_element_type=jnp.float32
    )
    input_lower, gain_one, shift_one = normalize_back(
        first_grad, first_plain, first_factor, norm_params[0]
    )
    input_grad = middle_grad + input_lower
    qkv_sum, out_sum = (
        lax.psum(qkv_part.astype(jnp.bfloat16), "dp").astype(jnp.float32),
        lax.psum(out_part, "dp").astype(jnp.float32),
    )
    leading = (lax.axis_index("dp") == 0).astype(jnp.float32)
    moments = [qkv_moment, out_moment, up_moment, down_moment]
    grads = [qkv_sum, out_sum, up_part, down_part]
    stats = jnp.stack(
        [
            squares_of(qkv_moment, qkv_sum, leading),
            squares_of(out_moment, out_sum, leading),
            squares_of(up_moment, up_part, 1.0),
            squares_of(down_moment, down_part, 1.0),
        ]
    )
    vector_part = jnp.stack([gain_one, shift_one, gain_two, shift_two])
    vector_sum, stat_sum = lax.psum((vector_part, stats), ("dp", "head"))
    grad_norm = jnp.sqrt(jnp.sum(stat_sum[:, 2]) + jnp.sum(vector_sum * vector_sum))
    clip = jnp.minimum(1.0, 1.0 / (grad_norm + 1e-06))
    sizes = jnp.sqrt(
        momentum_decay * momentum_decay * stat_sum[:, 0]
        + 2.0 * momentum_decay * clip * stat_sum[:, 1]
        + clip * clip * stat_sum[:, 2]
    )
    new_moments = [momentum_decay * moments[index] + clip * grads[index] for index in range(4)]
    starts = [
        (new_moments[index] / (sizes[index] + 1e-07)).astype(jnp.bfloat16) for index in range(4)
    ]
    up_block, down_block = (
        lax.all_gather(starts[2], "dp", axis=1, tiled=True),
        lax.all_gather(starts[3], "dp", axis=1, tiled=True),
    )
    blocks = [starts[0], starts[1], up_block, down_block]
    for turn in range(NS_STEPS):
        partials = (
            gram_left(blocks[0]),
            gram_right(blocks[1]),
            gram_left(blocks[2]),
            gram_left(blocks[3]),
        )
        grams = (
            lax.psum(partials[0].astype(jnp.bfloat16), "head").astype(jnp.float32),
            lax.psum(partials[1].astype(jnp.bfloat16), "head").astype(jnp.float32),
            lax.psum(partials[2].astype(jnp.bfloat16), "head").astype(jnp.float32),
            lax.psum(partials[3].astype(jnp.bfloat16), "head").astype(jnp.float32),
        )
        updated = []
        for index in range(4):
            gram = grams[index].astype(jnp.bfloat16)
            mix = (
                ns_b * gram.astype(jnp.float32)
                + ns_c * jnp.dot(gram, gram, preferred_element_type=jnp.float32)
            ).astype(jnp.bfloat16)
            if index == 1:
                product = jnp.dot(blocks[index], mix, preferred_element_type=jnp.float32)
            else:
                product = jnp.dot(mix, blocks[index], preferred_element_type=jnp.float32)
            updated.append(
                (ns_a * blocks[index].astype(jnp.float32) + product).astype(jnp.bfloat16)
            )
        blocks = updated
    share = up_weight.shape[1]
    offset = lax.axis_index("dp") * share
    owned = [
        blocks[0],
        blocks[1],
        lax.dynamic_slice_in_dim(blocks[2], offset, share, 1),
        lax.dynamic_slice_in_dim(blocks[3], offset, share, 1),
    ]
    weights = [qkv_weight, out_weight, up_weight, down_weight]
    factors = [
        math.sqrt(3.0),
        math.sqrt(SEQ / 8.0),
        math.sqrt(max(1.0, FF / width)),
        math.sqrt(max(1.0, FF / width)),
    ]
    new_weights = [
        weights[index] * (1.0 - muon_rate * muon_decay)
        - muon_rate * factors[index] * owned[index].astype(jnp.float32)
        for index in range(4)
    ]
    clipped = clip * vector_sum
    first_new = beta_one * norm_first + (1.0 - beta_one) * clipped
    second_new = beta_two * norm_second + (1.0 - beta_two) * clipped * clipped
    return (
        layer_out,
        input_grad,
        grad_norm,
        clipped,
        first_new,
        second_new,
        new_weights[0],
        new_moments[0],
        new_weights[1],
        new_moments[1],
        new_weights[2],
        new_moments[2],
        new_weights[3],
        new_moments[3],
    )


def solution(mesh):
    placed = (
        P(("dp", "head"), None),
        P("dp"),
        P(("dp", "head"), None),
        P(),
        P(),
        P(),
        P(None, "head"),
        P(None, "head"),
        P("head", None),
        P("head", None),
        P(None, ("dp", "head")),
        P(None, ("dp", "head")),
        P(None, ("dp", "head")),
        P(None, ("dp", "head")),
    )
    return jax.shard_map(
        shards,
        mesh=mesh,
        in_specs=placed,
        out_specs=(
            P(("dp", "head"), None),
            P(("dp", "head"), None),
            P(),
            P(),
            P(),
            P(),
            P(None, "head"),
            P(None, "head"),
            P("head", None),
            P("head", None),
            P(None, ("dp", "head")),
            P(None, ("dp", "head")),
            P(None, ("dp", "head")),
            P(None, ("dp", "head")),
        ),
        check_vma=False,
    )
```

profile of v0, /device:TPU:0, one launch (start us, length us, event | category | flops | bytes accessed | tf_op | source)
XLA Modules:
  0.0 1169.6 jit_solution(14758495943311568836)
XLA Ops:
  13.5 35.1 %all-gather.5.cloned.1.call-done = bf16[4096,512]{0,1:T(8,128)(2,1)} async-done(((bf16[1024,512]{0,1:T(8,128)(2,1)}), bf16[4096,512]{0,1:T(8,128)(2,1)}) %all-gather.5.cloned.1.call-update) | async-done | bytes 4194320 | tf_op jit(solution)/shard_map/all_gather | solution.py:123
  48.6 6.2 convolution_convert_fusion.2
  54.8 4.8 copy.76
  59.6 3.3 copy.103
  65.1 40.1 %while.22 = (s32[]{:T(128)}, bf16[8,512,2,64]{1,3,2,0:T(8,128)(2,1)}, f32[8,2,512,1]{2,1,3,0:T(2,128)}, bf16[8,512,2,64]{1,3,2,0:T(8,128)(2,1)}, s32[8,512]{1,0:...) while((s32[]{:T(128)}, ...), condition=%wide.region_5.6_spmd, body=%wide.region_2.5_spmd.sunk | while | flops 140835840 | bytes 7905881 | solution.py:132
  105.2 3.5 copy.80
  113.8 3.6 all-to-all-start
  118.9 17.6 %all_gather.22 = bf16[512,512]{1,0:T(8,128)(2,1)} all-gather(bf16[128,512]{1,0:T(8,128)(2,1)S(1)} %convert_element_type.448), channel_id=1, replica_groups=mesh['dp'=8,'head'=4] {'head'}, dimensions={0}, use_global_device_ids=true | all-gather | bytes 655360 | tf_op jit(solution)/shard_map/all_gather | solution.py:135
  140.3 8.4 multiply_convert_fusion.2
  148.7 18.5 %all-gather.9.cloned.1.call-done = bf16[512,2048]{0,1:T(8,128)(2,1)} async-done(((bf16[512,64]{0,1:T(8,128)(2,1)}), bf16[512,2048]{0,1:T(8,128)(2,1)}) %all-gather.9.cloned.1.call-update) | async-done | bytes 2097168 | tf_op jit(solution)/shard_map/all_gather | solution.py:142
  167.2 8.4 multiply_convert_fusion.1
  175.7 4.2 fusion.268
  182.8 3.0 multiply_reduce_fusion.1
  190.0 4.2 all-to-all-start.1
  197.5 11.2 all-to-all-done.1
  216.4 81.9 %while.23 = (s32[]{:T(128)}, bf16[8,512,2,3,64]{1,4,2,3,0:T(8,128)(2,1)}, bf16[8,512,2,64]{1,3,2,0:T(8,128)(2,1)}, s32[8,512]{1,0:T(8,128)}, bf16[8,512,2,64]{1,...) while((s32[]{:T(128)}, ...), condition=%wide.region_12.13_spmd, body=%wide.region_10.12_spmd.sunk | while | flops 342031360 | bytes 18380900 | solution.py:184
  298.4 3.7 copy.90
  305.4 3.1 convolution_convert_fusion.25
  309.2 7.3 fusion.263
  316.7 6.9 convolution_bitcast_fusion
  323.6 6.0 all_to_all.47
  329.7 4.6 copy.91
  334.2 4.8 all-to-all-start.2
  339.1 41.0 %all-reduce.14.cloned.1.call-done = (bf16[128,512]{1,0:T(8,128)(2,1)}, bf16[512,384]{1,0:T(8,128)(2,1)}) async-done(((bf16[128,512]{1,0:T(8,128)(2,1)}, bf16[512,384]{1,0:T(8,128)(2,1)}), (bf16[128,512]{1,0:T(8,128)(2,1)}, bf16[512,384]{1,0:T(8,128)(2,1)})) %all-reduce.14.cloned.1.call-update) | async-done | bytes 524304 | tf_op jit(solution)/shard_map/psum | solution.py:200
  388.8 12.2 %all-gather.11.cloned.1.call-done = bf16[512,1536]{1,0:T(8,128)(2,1)} async-done(((bf16[512,384]{1,0:T(8,128)(2,1)}), bf16[512,1536]{1,0:T(8,128)(2,1)}) %all-gather.11.cloned.1.call-update) | async-done | bytes 1572880 | tf_op jit(solution)/shard_map/all_gather | solution.py:190
  401.0 6.1 fusion.269
  413.6 130.7 %reduce-scatter.6.cloned.1.call-done = f32[512,64]{0,1:T(8,128)} async-done(((f32[512,2048]{0,1:T(8,128)}), f32[512,64]{0,1:T(8,128)}) %reduce-scatter.6.cloned.1.call-update) | async-done | bytes 131088 | tf_op jit(solution)/shard_map/reduce_scatter | solution.py:165
  545.9 137.6 %reduce-scatter.8.cloned.1.call-done = f32[512,64]{0,1:T(8,128)} async-done(((f32[512,2048]{0,1:T(8,128)}), f32[512,64]{0,1:T(8,128)}) %reduce-scatter.8.cloned.1.call-update) | async-done | bytes 131088 | tf_op jit(solution)/shard_map/reduce_scatter | solution.py:166
  685.2 4.0 maximum_bitcast_fusion
  690.4 37.2 %all-reduce = (f32[4,3]{1,0:T(4,128)S(1)}, f32[4,512]{1,0:T(4,128)}) all-reduce(f32[4,3]{1,0:T(4,128)} %pad_maximum_fusion.1, f32[4,512]{1,0:T(4,128)} %pad_maximum_fusion), channel_id=1, replica_groups=mesh['dp'=8,'head'=4] {'dp','head'}, use_global_device_ids=true, to_apply=%region_32.33 | all-reduce | flops 2060 | bytes 16480 | tf_op jit(solution)/shard_map/psum | solution.py:214
  737.7 31.5 %all_gather.27 = bf16[512,512]{0,1:T(8,128)(2,1)S(1)} all-gather(bf16[512,64]{0,1:T(8,128)(2,1)S(1)} %get-tuple-element.241), channel_id=1, replica_groups=mesh['dp'=8,'head'=4] {'dp'}, dimensions={1}, use_global_device_ids=true | all-gather | bytes 589824 | tf_op jit(solution)/shard_map/all_gather | solution.py:228
  772.0 31.2 %all_gather.26 = bf16[512,512]{0,1:T(8,128)(2,1)S(1)} all-gather(bf16[512,64]{0,1:T(8,128)(2,1)S(1)} %get-tuple-element.243), channel_id=1, replica_groups=mesh['dp'=8,'head'=4] {'dp'}, dimensions={1}, use_global_device_ids=true | all-gather | bytes 589824 | tf_op jit(solution)/shard_map/all_gather | solution.py:227
  808.4 51.9 %all-reduce.24.cloned.1.call-done = (bf16[512,512]{1,0:T(8,128)(2,1)}, bf16[512,512]{1,0:T(8,128)(2,1)}, bf16[512,512]{1,0:T(8,128)(2,1)}, bf16[512,512]{1,0:T(8,128)(2,1)}) async-done(((bf16[512,512]{1,0:T(8,128)(2,1)}, bf16[512,512]{1,0:T(8,128)(2,1)}, bf16[512,512]{1,0:T(8,128)(2,1)}, bf16[512,512]{1,0:T(8,128)(2,1)}), (bf16[512,512]{1,0:T(8,128)(2,1)}, bf16[512,512]{1,0:T(8,128)(2,1)}, ...) | async-done | bytes 2097168 | tf_op jit(solution)/shard_map/psum | solution.py:239
  860.3 3.5 fusion.100
  866.2 3.5 fusion.96
  879.5 52.1 %all-reduce.22.cloned.1.call-done = (bf16[512,512]{1,0:T(8,128)(2,1)}, bf16[512,512]{1,0:T(8,128)(2,1)}, bf16[512,512]{1,0:T(8,128)(2,1)}, bf16[512,512]{1,0:T(8,128)(2,1)}) async-done(((bf16[512,512]{1,0:T(8,128)(2,1)}, bf16[512,512]{1,0:T(8,128)(2,1)}, bf16[512,512]{1,0:T(8,128)(2,1)}, bf16[512,512]{1,0:T(8,128)(2,1)}), (bf16[512,512]{1,0:T(8,128)(2,1)}, bf16[512,512]{1,0:T(8,128)(2,1)}, ...) | async-done | bytes 2097168 | tf_op jit(solution)/shard_map/psum | solution.py:239
  931.6 3.5 fusion.101
  937.6 3.5 fusion.97
  953.8 52.1 %all-reduce.20.cloned.1.call-done = (bf16[512,512]{1,0:T(8,128)(2,1)}, bf16[512,512]{1,0:T(8,128)(2,1)}, bf16[512,512]{1,0:T(8,128)(2,1)}, bf16[512,512]{1,0:T(8,128)(2,1)}) async-done(((bf16[512,512]{1,0:T(8,128)(2,1)}, bf16[512,512]{1,0:T(8,128)(2,1)}, bf16[512,512]{1,0:T(8,128)(2,1)}, bf16[512,512]{1,0:T(8,128)(2,1)}), (bf16[512,512]{1,0:T(8,128)(2,1)}, bf16[512,512]{1,0:T(8,128)(2,1)}, ...) | async-done | bytes 2097168 | tf_op jit(solution)/shard_map/psum | solution.py:239
  1006.0 3.4 fusion.102
  1011.8 3.5 fusion.98
  1025.1 6.8 add_convert_fusion
  1034.8 42.2 %all-reduce.18.cloned.1.call-done = (bf16[512,512]{1,0:T(8,128)(2,1)}, bf16[512,512]{1,0:T(8,128)(2,1)}, bf16[512,512]{1,0:T(8,128)(2,1)}, bf16[512,512]{1,0:T(8,128)(2,1)}) async-done(((bf16[512,512]{1,0:T(8,128)(2,1)}, bf16[512,512]{1,0:T(8,128)(2,1)}, bf16[512,512]{1,0:T(8,128)(2,1)}, bf16[512,512]{1,0:T(8,128)(2,1)}), (bf16[512,512]{1,0:T(8,128)(2,1)}, bf16[512,512]{1,0:T(8,128)(2,1)}, ...) | async-done | bytes 2097168 | tf_op jit(solution)/shard_map/psum | solution.py:239
  1077.0 3.5 fusion.103
  1083.0 3.4 fusion.99
  1096.0 3.6 fusion.53
  1103.8 44.4 %all-reduce.16.cloned.1.call-done = (bf16[512,512]{1,0:T(8,128)(2,1)}, bf16[512,512]{1,0:T(8,128)(2,1)}, bf16[512,512]{1,0:T(8,128)(2,1)}, bf16[512,512]{1,0:T(8,128)(2,1)}) async-done(((bf16[512,512]{1,0:T(8,128)(2,1)}, bf16[512,512]{1,0:T(8,128)(2,1)}, bf16[512,512]{1,0:T(8,128)(2,1)}, bf16[512,512]{1,0:T(8,128)(2,1)}), (bf16[512,512]{1,0:T(8,128)(2,1)}, bf16[512,512]{1,0:T(8,128)(2,1)}, ...) | async-done | bytes 2097168 | tf_op jit(solution)/shard_map/psum | solution.py:239
  1148.2 3.2 fusion.112
  (354 shorter events, 264.9 us)
Async XLA Ops:
  7.2 41.4 %all-gather.5.cloned.1.call-start = ((), (), s32[]{:S(2)}) async-start(), calls=%async_computation.6 | async-start | bytes 5242880 | tf_op jit(solution)/shard_map/all_gather | solution.py:123
  8.9 3.1 copy-start.26
  9.3 3.5 copy-start.13
  11.3 128.7 %all-gather.7.cloned.1.call-start = ((), (), s32[]{:S(2)}) async-start(), calls=%async_computation.7 | async-start | bytes 2162688 | tf_op jit(solution)/shard_map/all_gather | solution.py:141
  12.0 155.2 %all-gather.9.cloned.1.call-start = ((), (), s32[]{:S(2)}) async-start(), calls=%async_computation.8 | async-start | bytes 2162688 | tf_op jit(solution)/shard_map/all_gather | solution.py:142
  12.8 42.0 %copy-start.10 = (bf16[512,384]{1,0:T(8,128)(2,1)}, bf16[512,384]{1,0:T(8,128)(2,1)S(1)}, u32[]{:S(2)}) copy-start(bf16[512,384]{1,0:T(8,128)(2,1)S(1)} %convert_element_type.446) | copy-start | bytes 1179652
  105.2 6.1 copy-start.4
  105.2 6.1 copy-start.5
  111.2 6.2 copy-start.30
  113.8 3.7 copy-start.11
  113.8 22.7 %all-to-all-start = ((bf16[4,1024,128]{1,2,0:T(8,128)(2,1)}), bf16[4,1024,128]{1,2,0:T(8,128)(2,1)S(1)}, u32[]{:S(2)}, u32[]{:S(2)}) async-start(bf16[4,1024,128]{1,2,0:T(8,128)(2,1)} %copy.81), calls=%async_computation | async-start | bytes 2097152 | tf_op jit(solution)/shard_map/all_to_all | solution.py:134
  139.6 43.2 %copy-start = (f32[1024,512]{0,1:T(8,128)}, f32[1024,512]{0,1:T(8,128)S(1)}, u32[]{:S(2)}) copy-start(f32[1024,512]{0,1:T(8,128)S(1)} %get-tuple-element.263) | copy-start | bytes 6291460
  167.2 8.4 copy-start.49
  175.7 4.2 copy-start.51
  182.8 3.0 copy-start.7
  190.0 18.8 %all-to-all-start.1 = ((bf16[1024,4,128]{0,2,1:T(8,128)(2,1)}), bf16[1024,4,128]{0,2,1:T(8,128)(2,1)}, u32[]{:S(2)}, u32[]{:S(2)}) async-start(bf16[1024,4,128]{0,2,1:T(8,128)(2,1)} %bitcast.284), calls=%async_computation.1 | async-start | bytes 2097152 | tf_op jit(solution)/shard_map/all_to_all | solution.py:176
  194.2 114.3 %reduce-scatter.4.cloned.1.call-start = ((), (), s32[]{:S(2)}) async-start(), calls=%async_computation.10 | async-start | bytes 655360 | tf_op jit(solution)/shard_map/reduce_scatter | solution.py:180
  197.1 183.1 %all-reduce.14.cloned.1.call-start = ((), (), s32[]{:S(2)}) async-start(), calls=%async_computation.13 | async-start | bytes 1048576 | tf_op jit(solution)/shard_map/psum | solution.py:200
  302.1 3.3 copy-start.48
  308.6 92.4 %all-gather.11.cloned.1.call-start = ((), (), s32[]{:S(2)}) async-start(), calls=%async_computation.9 | async-start | bytes 1966080 | tf_op jit(solution)/shard_map/all_gather | solution.py:190
  309.1 235.2 %reduce-scatter.6.cloned.1.call-start = ((), (), s32[]{:S(2)}) async-start(), calls=%async_computation.11 | async-start | bytes 4325376 | tf_op jit(solution)/shard_map/reduce_scatter | solution.py:165
  316.5 367.0 %reduce-scatter.8.cloned.1.call-start = ((), (), s32[]{:S(2)}) async-start(), calls=%async_computation.12 | async-start | bytes 4325376 | tf_op jit(solution)/shard_map/reduce_scatter | solution.py:166
  334.2 50.5 %copy-start.12 = (f32[128,512]{1,0:T(8,128)S(1)}, f32[128,512]{1,0:T(8,128)}, u32[]{:S(2)}) copy-start(f32[128,512]{1,0:T(8,128)} %param.27) | copy-start | bytes 786436
  334.2 66.8 %all-to-all-start.2 = ((bf16[4,1024,384]{1,2,0:T(8,128)(2,1)}), bf16[4,1024,384]{1,2,0:T(8,128)(2,1)}, u32[]{:S(2)}, u32[]{:S(2)}) async-start(bf16[4,1024,384]{1,2,0:T(8,128)(2,1)} %copy.91), calls=%async_computation.2 | async-start | bytes 6291456 | tf_op jit(solution)/shard_map/all_to_all | solution.py:189
  339.1 521.2 %all-reduce.24.cloned.1.call-start = ((), (), s32[]{:S(2)}) async-start(), calls=%async_computation.18 | async-start | bytes 4194304 | tf_op jit(solution)/shard_map/psum | solution.py:239
  410.0 322.7 %copy-start.8 = (bf16[512,384]{1,0:T(8,128)(2,1)S(1)}, bf16[512,384]{1,0:T(8,128)(2,1)}, u32[]{:S(2)}) copy-start(bf16[512,384]{1,0:T(8,128)(2,1)} %get-tuple-element.220) | copy-start | bytes 1179652
  734.8 36.5 %copy-start.22 = (f32[512,64]{0,1:T(8,128)S(1)}, f32[512,64]{0,1:T(8,128)}, u32[]{:S(2)}) copy-start(f32[512,64]{0,1:T(8,128)} %param.29) | copy-start | bytes 393220
  734.8 36.5 %copy-start.23 = (f32[512,64]{0,1:T(8,128)S(1)}, f32[512,64]{0,1:T(8,128)}, u32[]{:S(2)}) copy-start(f32[512,64]{0,1:T(8,128)} %reduce-scatter.6.cloned.1.call-done) | copy-start | bytes 393220
  769.3 35.2 %copy-start.24 = (bf16[512,512]{0,1:T(8,128)(2,1)}, bf16[512,512]{0,1:T(8,128)(2,1)S(1)}, u32[]{:S(2)}) copy-start(bf16[512,512]{0,1:T(8,128)(2,1)S(1)} %all_gather.27) | copy-start | bytes 1572868
  769.3 36.5 %copy-start.32 = (f32[128,512]{1,0:T(8,128)S(1)}, f32[128,512]{1,0:T(8,128)}, u32[]{:S(2)}) copy-start(f32[128,512]{1,0:T(8,128)} %fusion.219) | copy-start | bytes 786436
  770.5 36.3 %copy-start.15 = (f32[512,384]{1,0:T(8,128)S(1)}, f32[512,384]{1,0:T(8,128)}, u32[]{:S(2)}) copy-start(f32[512,384]{1,0:T(8,128)} %fusion.174) | copy-start | bytes 2359300
  808.2 123.5 %all-reduce.22.cloned.1.call-start = ((), (), s32[]{:S(2)}) async-start(), calls=%async_computation.17 | async-start | bytes 4194304 | tf_op jit(solution)/shard_map/psum | solution.py:239
  866.2 6.0 copy-start.33
  879.5 126.5 %all-reduce.20.cloned.1.call-start = ((), (), s32[]{:S(2)}) async-start(), calls=%async_computation.16 | async-start | bytes 4194304 | tf_op jit(solution)/shard_map/psum | solution.py:239
  953.8 123.2 %all-reduce.18.cloned.1.call-start = ((), (), s32[]{:S(2)}) async-start(), calls=%async_computation.15 | async-start | bytes 4194304 | tf_op jit(solution)/shard_map/psum | solution.py:239
  1011.8 6.0 copy-start.21
  1023.5 8.4 copy-start.9
  1024.8 123.3 %all-reduce.16.cloned.1.call-start = ((), (), s32[]{:S(2)}) async-start(), calls=%async_computation.14 | async-start | bytes 4194304 | tf_op jit(solution)/shard_map/psum | solution.py:239
  1083.0 5.9 copy-start.19
  1099.6 3.6 copy-start.40
  1099.6 48.6 %copy-start.42 = (bf16[512,512]{0,1:T(8,128)(2,1)S(1)}, bf16[512,512]{0,1:T(8,128)(2,1)}, u32[]{:S(2)}) copy-start(bf16[512,512]{0,1:T(8,128)(2,1)} %fusion.103) | copy-start | bytes 1572868
  1102.6 48.8 %copy-start.43 = (bf16[512,512]{0,1:T(8,128)(2,1)S(1)}, bf16[512,512]{0,1:T(8,128)(2,1)}, u32[]{:S(2)}) copy-start(bf16[512,512]{0,1:T(8,128)(2,1)} %fusion.99) | copy-start | bytes 1572868
  1103.2 50.5 %copy-start.34 = (f32[4,512]{1,0:T(4,128)}, f32[4,512]{1,0:T(4,128)S(1)}, u32[]{:S(2)}) copy-start(f32[4,512]{1,0:T(4,128)S(1)} %get-tuple-element.246) | copy-start | bytes 24580
  1151.4 4.0 copy-start.29
  1151.4 5.6 copy-start.17
  1151.4 5.6 copy-start.31
  1153.7 6.1 copy-start.14
  1155.4 4.4 copy-start.50
  (20 other events, 42.1 us)
Sparse Core Ops, SparseCore 0:
  11.4 37.1 all-gather.4
  52.0 56.3 all-gather.6
  111.9 55.3 all-gather.8
  197.8 21.8 reduce-scatter.3
  308.7 71.3 all-reduce.13
  382.1 18.8 all-gather.10
  403.3 140.9 reduce-scatter.5
  546.6 136.9 reduce-scatter.7
  808.3 51.9 all-reduce.23
  879.6 51.9 all-reduce.21
  953.9 52.0 all-reduce.19
  1025.0 51.9 all-reduce.17
  1096.1 52.0 all-reduce.15
where the time goes:
time: 1180 us; the launch traced here: 1170 us
  waiting for transfers between devices  630 us (53%)
  matrix products  239 us (20%)
  blocking collectives  118 us (10%)
  local copies, waits for them, and re-layouts  78.6 us (7%)
  other arithmetic  69.6 us (6%)
  between operations  20.1 us (2%)
  starting transfers between devices  14.3 us (1%)
    psum x5, waiting for transfers between devices, shards(): lax.psum(partials[0].astype(jnp.bfloat16), 'head').astype(jnp.float32)  243 us
    reduce_scatter x1, waiting for transfers between devices, shards(): lax.psum_scatter(down_grad, ('dp', 'head'), scatter_dimension=1, tiled=True)  138 us
    reduce_scatter x1, waiting for transfers between devices, shards(): lax.psum_scatter(up_grad, ('dp', 'head'), scatter_dimension=1, tiled=True)  131 us
    dot_general x15, matrix products, shards(): product = jnp.dot(mix, blocks[index], preferred_element_type=jnp.float32)  45.7 us
    psum x1, waiting for transfers between devices, shards(): lax.psum(out_part, 'dp').astype(jnp.float32)  41 us
    psum x1, blocking collectives, shards(): vector_sum, stat_sum = lax.psum((vector_part, stats), ('dp', 'head'))  37.2 us
    all_gather x1, waiting for transfers between devices, shards(): lax.all_gather(first.astype(jnp.bfloat16), 'head', axis=0, tiled=True)  35.1 us
    all_gather x1, blocking collectives, shards(): lax.all_gather(starts[3], 'dp', axis=1, tiled=True)  31.5 us
  transfers between devices with their start and end apart: 16, of which 12 were waited for; matrix products, arithmetic and copies ran while one was open for 20% of the time, Pallas kernels for 0%

commit v1 on v0

--- a/solution.py
+++ b/solution.py
@@ -3,6 +3,7 @@
 import jax.numpy as jnp
 from jax import lax
 from jax.sharding import PartitionSpec as P
+from jax.lax import psum
 
 HEAD_DIM = 64
 FF = 2048
@@ -211,7 +212,7 @@
         ]
     )
     vector_part = jnp.stack([gain_one, shift_one, gain_two, shift_two])
-    vector_sum, stat_sum = lax.psum((vector_part, stats), ("dp", "head"))
+    vector_sum, stat_sum = psum(psum((vector_part, stats), axis_name="head"), axis_name="dp")
     grad_norm = jnp.sqrt(jnp.sum(stat_sum[:, 2]) + jnp.sum(vector_sum * vector_sum))
     clip = jnp.minimum(1.0, 1.0 / (grad_norm + 1e-06))
     sizes = jnp.sqrt(

time: 1180 us -> 1190 us (level)
    psum x1 -> x2, blocking collectives: 37.2 us -> 44.7 us  [the longest x1 33.4 us: shards(): psum(psum((vector_part, stats), axis_name='head'), axis_name='dp')]
where the time goes in v1:
time: 1190 us; the launch traced here: 1170 us
  waiting for transfers between devices  625 us (53%)
  matrix products  246 us (21%)
  blocking collectives  124 us (10%)
  local copies, waits for them, and re-layouts  72.8 us (6%)
  other arithmetic  69.1 us (6%)
  between operations  20.2 us (2%)
  starting transfers between devices  14.3 us (1%)
    psum x5, waiting for transfers between devices, shards(): lax.psum(partials[0].astype(jnp.bfloat16), 'head').astype(jnp.float32)  239 us
    reduce_scatter x1, waiting for transfers between devices, shards(): lax.psum_scatter(down_grad, ('dp', 'head'), scatter_dimension=1, tiled=True)  138 us
    reduce_scatter x1, waiting for transfers between devices, shards(): lax.psum_scatter(up_grad, ('dp', 'head'), scatter_dimension=1, tiled=True)  131 us
    dot_general x15, matrix products, shards(): product = jnp.dot(mix, blocks[index], preferred_element_type=jnp.float32)  45.7 us
    psum x1, waiting for transfers between devices, shards(): lax.psum(out_part, 'dp').astype(jnp.float32)  41 us
    all_gather x1, waiting for transfers between devices, shards(): lax.all_gather(first.astype(jnp.bfloat16), 'head', axis=0, tiled=True)  35.7 us
    psum x1, blocking collectives, shards(): psum(psum((vector_part, stats), axis_name='head'), axis_name='dp')  33.4 us
    all_gather x1, blocking collectives, shards(): lax.all_gather(starts[3], 'dp', axis=1, tiled=True)  31.5 us
  transfers between devices with their start and end apart: 16, of which 12 were waited for; matrix products, arithmetic and copies ran while one was open for 20% of the time, Pallas kernels for 0%

profile of v1, /device:TPU:0, one launch (start us, length us, event | category | flops | bytes accessed | tf_op | source)
XLA Modules:
  0.0 1173.1 jit_solution(11436717354638160790)
XLA Ops:
  12.9 35.7 %all-gather.5.cloned.1.call-done = bf16[4096,512]{0,1:T(8,128)(2,1)} async-done(((bf16[1024,512]{0,1:T(8,128)(2,1)}), bf16[4096,512]{0,1:T(8,128)(2,1)}) %all-gather.5.cloned.1.call-update) | async-done | bytes 4194320 | tf_op jit(solution)/shard_map/all_gather | solution.py:124
  48.6 6.2 convolution_convert_fusion.2
  54.8 4.8 copy.76
  59.6 3.3 copy.103
  66.1 41.6 %while.22 = (s32[]{:T(128)}, bf16[8,512,2,64]{1,3,2,0:T(8,128)(2,1)}, f32[8,2,512,1]{2,1,3,0:T(2,128)}, bf16[8,512,2,64]{1,3,2,0:T(8,128)(2,1)}, s32[8,512]{1,0:...) while((s32[]{:T(128)}, ...), condition=%wide.region_5.6_spmd, body=%wide.region_2.5_spmd.sunk | while | flops 140835840 | bytes 7905881 | solution.py:133
  107.7 3.2 copy.80
  115.9 3.7 all-to-all-start
  121.0 17.2 %all_gather.22 = bf16[512,512]{1,0:T(8,128)(2,1)} all-gather(bf16[128,512]{1,0:T(8,128)(2,1)S(1)} %convert_element_type.448), channel_id=1, replica_groups=mesh['dp'=8,'head'=4] {'head'}, dimensions={0}, use_global_device_ids=true | all-gather | bytes 655360 | tf_op jit(solution)/shard_map/all_gather | solution.py:136
  142.0 8.4 multiply_convert_fusion.2
  150.5 16.7 %all-gather.9.cloned.1.call-done = bf16[512,2048]{0,1:T(8,128)(2,1)} async-done(((bf16[512,64]{0,1:T(8,128)(2,1)}), bf16[512,2048]{0,1:T(8,128)(2,1)}) %all-gather.9.cloned.1.call-update) | async-done | bytes 2097168 | tf_op jit(solution)/shard_map/all_gather | solution.py:143
  167.2 8.4 multiply_convert_fusion.1
  175.6 4.2 fusion.268
  189.9 4.2 all-to-all-start.1
  197.4 11.2 all-to-all-done.1
  216.4 81.9 %while.23 = (s32[]{:T(128)}, bf16[8,512,2,3,64]{1,4,2,3,0:T(8,128)(2,1)}, bf16[8,512,2,64]{1,3,2,0:T(8,128)(2,1)}, s32[8,512]{1,0:T(8,128)}, bf16[8,512,2,64]{1,...) while((s32[]{:T(128)}, ...), condition=%wide.region_12.13_spmd, body=%wide.region_10.12_spmd.sunk | while | flops 342031360 | bytes 18380900 | solution.py:185
  298.3 3.7 copy.90
  305.3 3.1 convolution_convert_fusion.25
  309.1 7.3 fusion.263
  316.7 6.9 convolution_bitcast_fusion
  323.5 6.0 all_to_all.47
  329.6 4.6 copy.91
  334.2 4.8 all-to-all-start.2
  339.1 41.0 %all-reduce.15.cloned.1.call-done = (bf16[128,512]{1,0:T(8,128)(2,1)}, bf16[512,384]{1,0:T(8,128)(2,1)}) async-done(((bf16[128,512]{1,0:T(8,128)(2,1)}, bf16[512,384]{1,0:T(8,128)(2,1)}), (bf16[128,512]{1,0:T(8,128)(2,1)}, bf16[512,384]{1,0:T(8,128)(2,1)})) %all-reduce.15.cloned.1.call-update) | async-done | bytes 524304 | tf_op jit(solution)/shard_map/psum | solution.py:201
  388.8 12.2 %all-gather.11.cloned.1.call-done = bf16[512,1536]{1,0:T(8,128)(2,1)} async-done(((bf16[512,384]{1,0:T(8,128)(2,1)}), bf16[512,1536]{1,0:T(8,128)(2,1)}) %all-gather.11.cloned.1.call-update) | async-done | bytes 1572880 | tf_op jit(solution)/shard_map/all_gather | solution.py:191
  401.0 6.1 fusion.269
  413.0 131.2 %reduce-scatter.6.cloned.1.call-done = f32[512,64]{0,1:T(8,128)} async-done(((f32[512,2048]{0,1:T(8,128)}), f32[512,64]{0,1:T(8,128)}) %reduce-scatter.6.cloned.1.call-update) | async-done | bytes 131088 | tf_op jit(solution)/shard_map/reduce_scatter | solution.py:166
  545.8 137.6 %reduce-scatter.8.cloned.1.call-done = f32[512,64]{0,1:T(8,128)} async-done(((f32[512,2048]{0,1:T(8,128)}), f32[512,64]{0,1:T(8,128)}) %reduce-scatter.8.cloned.1.call-update) | async-done | bytes 131088 | tf_op jit(solution)/shard_map/reduce_scatter | solution.py:167
  685.0 4.0 maximum_bitcast_fusion
  690.2 11.2 all-reduce.1
  701.4 33.4 %all-reduce = (f32[4,3]{1,0:T(4,128)S(1)}, f32[4,512]{1,0:T(4,128)}) all-reduce(f32[4,3]{1,0:T(4,128)} %get-tuple-element.219, f32[4,512]{1,0:T(4,128)} %get-tuple-element.220), channel_id=1, replica_groups=mesh['dp'=8,'head'=4] {'dp'}, use_global_device_ids=true, to_apply=%region_33.34 | all-reduce | flops 2060 | bytes 16480 | tf_op jit(solution)/shard_map/psum | solution.py:215
  745.0 31.5 %all_gather.27 = bf16[512,512]{0,1:T(8,128)(2,1)S(1)} all-gather(bf16[512,64]{0,1:T(8,128)(2,1)S(1)} %get-tuple-element.243), channel_id=1, replica_groups=mesh['dp'=8,'head'=4] {'dp'}, dimensions={1}, use_global_device_ids=true | all-gather | bytes 589824 | tf_op jit(solution)/shard_map/all_gather | solution.py:229
  779.2 31.2 %all_gather.26 = bf16[512,512]{0,1:T(8,128)(2,1)S(1)} all-gather(bf16[512,64]{0,1:T(8,128)(2,1)S(1)} %get-tuple-element.245), channel_id=1, replica_groups=mesh['dp'=8,'head'=4] {'dp'}, dimensions={1}, use_global_device_ids=true | all-gather | bytes 589824 | tf_op jit(solution)/shard_map/all_gather | solution.py:228
  815.6 48.2 %all-reduce.25.cloned.1.call-done = (bf16[512,512]{1,0:T(8,128)(2,1)}, bf16[512,512]{1,0:T(8,128)(2,1)}, bf16[512,512]{1,0:T(8,128)(2,1)}, bf16[512,512]{1,0:T(8,128)(2,1)}) async-done(((bf16[512,512]{1,0:T(8,128)(2,1)}, bf16[512,512]{1,0:T(8,128)(2,1)}, bf16[512,512]{1,0:T(8,128)(2,1)}, bf16[512,512]{1,0:T(8,128)(2,1)}), (bf16[512,512]{1,0:T(8,128)(2,1)}, bf16[512,512]{1,0:T(8,128)(2,1)}, ...) | async-done | bytes 2097168 | tf_op jit(solution)/shard_map/psum | solution.py:240
  863.8 3.5 fusion.100
  869.7 3.5 fusion.96
  883.0 52.1 %all-reduce.23.cloned.1.call-done = (bf16[512,512]{1,0:T(8,128)(2,1)}, bf16[512,512]{1,0:T(8,128)(2,1)}, bf16[512,512]{1,0:T(8,128)(2,1)}, bf16[512,512]{1,0:T(8,128)(2,1)}) async-done(((bf16[512,512]{1,0:T(8,128)(2,1)}, bf16[512,512]{1,0:T(8,128)(2,1)}, bf16[512,512]{1,0:T(8,128)(2,1)}, bf16[512,512]{1,0:T(8,128)(2,1)}), (bf16[512,512]{1,0:T(8,128)(2,1)}, bf16[512,512]{1,0:T(8,128)(2,1)}, ...) | async-done | bytes 2097168 | tf_op jit(solution)/shard_map/psum | solution.py:240
  935.1 3.5 fusion.101
  941.1 3.5 fusion.97
  957.3 52.1 %all-reduce.21.cloned.1.call-done = (bf16[512,512]{1,0:T(8,128)(2,1)}, bf16[512,512]{1,0:T(8,128)(2,1)}, bf16[512,512]{1,0:T(8,128)(2,1)}, bf16[512,512]{1,0:T(8,128)(2,1)}) async-done(((bf16[512,512]{1,0:T(8,128)(2,1)}, bf16[512,512]{1,0:T(8,128)(2,1)}, bf16[512,512]{1,0:T(8,128)(2,1)}, bf16[512,512]{1,0:T(8,128)(2,1)}), (bf16[512,512]{1,0:T(8,128)(2,1)}, bf16[512,512]{1,0:T(8,128)(2,1)}, ...) | async-done | bytes 2097168 | tf_op jit(solution)/shard_map/psum | solution.py:240
  1009.4 3.4 fusion.102
  1015.3 3.5 fusion.98
  1028.6 6.8 add_convert_fusion
  1038.3 42.2 %all-reduce.19.cloned.1.call-done = (bf16[512,512]{1,0:T(8,128)(2,1)}, bf16[512,512]{1,0:T(8,128)(2,1)}, bf16[512,512]{1,0:T(8,128)(2,1)}, bf16[512,512]{1,0:T(8,128)(2,1)}) async-done(((bf16[512,512]{1,0:T(8,128)(2,1)}, bf16[512,512]{1,0:T(8,128)(2,1)}, bf16[512,512]{1,0:T(8,128)(2,1)}, bf16[512,512]{1,0:T(8,128)(2,1)}), (bf16[512,512]{1,0:T(8,128)(2,1)}, bf16[512,512]{1,0:T(8,128)(2,1)}, ...) | async-done | bytes 2097168 | tf_op jit(solution)/shard_map/psum | solution.py:240
  1080.5 3.5 fusion.103
  1086.5 3.4 fusion.99
  1099.5 3.6 fusion.53
  1107.3 44.4 %all-reduce.17.cloned.1.call-done = (bf16[512,512]{1,0:T(8,128)(2,1)}, bf16[512,512]{1,0:T(8,128)(2,1)}, bf16[512,512]{1,0:T(8,128)(2,1)}, bf16[512,512]{1,0:T(8,128)(2,1)}) async-done(((bf16[512,512]{1,0:T(8,128)(2,1)}, bf16[512,512]{1,0:T(8,128)(2,1)}, bf16[512,512]{1,0:T(8,128)(2,1)}, bf16[512,512]{1,0:T(8,128)(2,1)}), (bf16[512,512]{1,0:T(8,128)(2,1)}, bf16[512,512]{1,0:T(8,128)(2,1)}, ...) | async-done | bytes 2097168 | tf_op jit(solution)/shard_map/psum | solution.py:240
  1151.6 3.2 fusion.112
  (359 shorter events, 269.2 us)
Async XLA Ops:
  7.2 41.4 %all-gather.5.cloned.1.call-start = ((), (), s32[]{:S(2)}) async-start(), calls=%async_computation.6 | async-start | bytes 5242880 | tf_op jit(solution)/shard_map/all_gather | solution.py:124
  8.9 3.1 copy-start.25
  9.3 3.5 copy-start.12
  9.9 400.1 %copy-start.36 = (f32[1,512]{1,0:T(1,128)}, f32[1,512]{1,0:T(1,128)S(1)}, u32[]{:S(2)}) copy-start(f32[1,512]{1,0:T(1,128)S(1)} %get-tuple-element.258) | copy-start | bytes 6148
  11.3 130.4 %all-gather.7.cloned.1.call-start = ((), (), s32[]{:S(2)}) async-start(), calls=%async_computation.7 | async-start | bytes 2162688 | tf_op jit(solution)/shard_map/all_gather | solution.py:142
  12.0 155.1 %all-gather.9.cloned.1.call-start = ((), (), s32[]{:S(2)}) async-start(), calls=%async_computation.8 | async-start | bytes 2162688 | tf_op jit(solution)/shard_map/all_gather | solution.py:143
  12.8 42.0 %copy-start.9 = (bf16[512,384]{1,0:T(8,128)(2,1)}, bf16[512,384]{1,0:T(8,128)(2,1)S(1)}, u32[]{:S(2)}) copy-start(bf16[512,384]{1,0:T(8,128)(2,1)S(1)} %convert_element_type.446) | copy-start | bytes 1179652
  107.7 5.7 copy-start.4
  107.7 5.7 copy-start.33
  113.4 6.2 copy-start.29
  115.9 3.7 copy-start.10
  115.9 22.3 %all-to-all-start = ((bf16[4,1024,128]{1,2,0:T(8,128)(2,1)}), bf16[4,1024,128]{1,2,0:T(8,128)(2,1)S(1)}, u32[]{:S(2)}, u32[]{:S(2)}) async-start(bf16[4,1024,128]{1,2,0:T(8,128)(2,1)} %copy.81), calls=%async_computation | async-start | bytes 2097152 | tf_op jit(solution)/shard_map/all_to_all | solution.py:135
  141.3 41.4 %copy-start = (f32[1024,512]{0,1:T(8,128)}, f32[1024,512]{0,1:T(8,128)S(1)}, u32[]{:S(2)}) copy-start(f32[1024,512]{0,1:T(8,128)S(1)} %get-tuple-element.265) | copy-start | bytes 6291460
  167.2 8.4 copy-start.51
  175.6 4.2 copy-start.53
  189.9 18.8 %all-to-all-start.1 = ((bf16[1024,4,128]{0,2,1:T(8,128)(2,1)}), bf16[1024,4,128]{0,2,1:T(8,128)(2,1)}, u32[]{:S(2)}, u32[]{:S(2)}) async-start(bf16[1024,4,128]{0,2,1:T(8,128)(2,1)} %bitcast.284), calls=%async_computation.1 | async-start | bytes 2097152 | tf_op jit(solution)/shard_map/all_to_all | solution.py:177
  194.1 114.3 %reduce-scatter.4.cloned.1.call-start = ((), (), s32[]{:S(2)}) async-start(), calls=%async_computation.10 | async-start | bytes 655360 | tf_op jit(solution)/shard_map/reduce_scatter | solution.py:181
  197.0 183.1 %all-reduce.15.cloned.1.call-start = ((), (), s32[]{:S(2)}) async-start(), calls=%async_computation.13 | async-start | bytes 1048576 | tf_op jit(solution)/shard_map/psum | solution.py:201
  302.0 3.3 copy-start.50
  308.5 92.5 %all-gather.11.cloned.1.call-start = ((), (), s32[]{:S(2)}) async-start(), calls=%async_computation.9 | async-start | bytes 1966080 | tf_op jit(solution)/shard_map/all_gather | solution.py:191
  309.0 235.1 %reduce-scatter.6.cloned.1.call-start = ((), (), s32[]{:S(2)}) async-start(), calls=%async_computation.11 | async-start | bytes 4325376 | tf_op jit(solution)/shard_map/reduce_scatter | solution.py:166
  316.4 366.9 %reduce-scatter.8.cloned.1.call-start = ((), (), s32[]{:S(2)}) async-start(), calls=%async_computation.12 | async-start | bytes 4325376 | tf_op jit(solution)/shard_map/reduce_scatter | solution.py:167
  334.1 50.5 %copy-start.11 = (f32[128,512]{1,0:T(8,128)S(1)}, f32[128,512]{1,0:T(8,128)}, u32[]{:S(2)}) copy-start(f32[128,512]{1,0:T(8,128)} %param.27) | copy-start | bytes 786436
  334.2 66.8 %all-to-all-start.2 = ((bf16[4,1024,384]{1,2,0:T(8,128)(2,1)}), bf16[4,1024,384]{1,2,0:T(8,128)(2,1)}, u32[]{:S(2)}, u32[]{:S(2)}) async-start(bf16[4,1024,384]{1,2,0:T(8,128)(2,1)} %copy.91), calls=%async_computation.2 | async-start | bytes 6291456 | tf_op jit(solution)/shard_map/all_to_all | solution.py:190
  339.0 524.8 %all-reduce.25.cloned.1.call-start = ((), (), s32[]{:S(2)}) async-start(), calls=%async_computation.18 | async-start | bytes 4194304 | tf_op jit(solution)/shard_map/psum | solution.py:240
  410.0 330.0 %copy-start.7 = (bf16[512,384]{1,0:T(8,128)(2,1)S(1)}, bf16[512,384]{1,0:T(8,128)(2,1)}, u32[]{:S(2)}) copy-start(bf16[512,384]{1,0:T(8,128)(2,1)} %get-tuple-element.222) | copy-start | bytes 1179652
  742.1 36.4 %copy-start.21 = (f32[512,64]{0,1:T(8,128)S(1)}, f32[512,64]{0,1:T(8,128)}, u32[]{:S(2)}) copy-start(f32[512,64]{0,1:T(8,128)} %param.29) | copy-start | bytes 393220
  742.1 36.4 %copy-start.22 = (f32[512,64]{0,1:T(8,128)S(1)}, f32[512,64]{0,1:T(8,128)}, u32[]{:S(2)}) copy-start(f32[512,64]{0,1:T(8,128)} %reduce-scatter.6.cloned.1.call-done) | copy-start | bytes 393220
  776.5 35.1 %copy-start.23 = (bf16[512,512]{0,1:T(8,128)(2,1)}, bf16[512,512]{0,1:T(8,128)(2,1)S(1)}, u32[]{:S(2)}) copy-start(bf16[512,512]{0,1:T(8,128)(2,1)S(1)} %all_gather.27) | copy-start | bytes 1572868
  776.5 36.4 %copy-start.31 = (f32[128,512]{1,0:T(8,128)S(1)}, f32[128,512]{1,0:T(8,128)}, u32[]{:S(2)}) copy-start(f32[128,512]{1,0:T(8,128)} %fusion.219) | copy-start | bytes 786436
  777.8 36.3 %copy-start.14 = (f32[512,384]{1,0:T(8,128)S(1)}, f32[512,384]{1,0:T(8,128)}, u32[]{:S(2)}) copy-start(f32[512,384]{1,0:T(8,128)} %fusion.174) | copy-start | bytes 2359300
  815.4 119.7 %all-reduce.23.cloned.1.call-start = ((), (), s32[]{:S(2)}) async-start(), calls=%async_computation.17 | async-start | bytes 4194304 | tf_op jit(solution)/shard_map/psum | solution.py:240
  869.7 6.0 copy-start.32
  882.9 126.5 %all-reduce.21.cloned.1.call-start = ((), (), s32[]{:S(2)}) async-start(), calls=%async_computation.16 | async-start | bytes 4194304 | tf_op jit(solution)/shard_map/psum | solution.py:240
  957.3 123.2 %all-reduce.19.cloned.1.call-start = ((), (), s32[]{:S(2)}) async-start(), calls=%async_computation.15 | async-start | bytes 4194304 | tf_op jit(solution)/shard_map/psum | solution.py:240
  1015.3 6.0 copy-start.20
  1027.0 8.4 copy-start.8
  1028.3 123.3 %all-reduce.17.cloned.1.call-start = ((), (), s32[]{:S(2)}) async-start(), calls=%async_computation.14 | async-start | bytes 4194304 | tf_op jit(solution)/shard_map/psum | solution.py:240
  1086.5 5.9 copy-start.18
  1103.1 3.6 copy-start.42
  1103.1 48.6 %copy-start.44 = (bf16[512,512]{0,1:T(8,128)(2,1)S(1)}, bf16[512,512]{0,1:T(8,128)(2,1)}, u32[]{:S(2)}) copy-start(bf16[512,512]{0,1:T(8,128)(2,1)} %fusion.103) | copy-start | bytes 1572868
  1106.0 48.8 %copy-start.45 = (bf16[512,512]{0,1:T(8,128)(2,1)S(1)}, bf16[512,512]{0,1:T(8,128)(2,1)}, u32[]{:S(2)}) copy-start(bf16[512,512]{0,1:T(8,128)(2,1)} %fusion.99) | copy-start | bytes 1572868
  1106.7 50.5 %copy-start.34 = (f32[4,512]{1,0:T(4,128)}, f32[4,512]{1,0:T(4,128)S(1)}, u32[]{:S(2)}) copy-start(f32[4,512]{1,0:T(4,128)S(1)} %get-tuple-element.248) | copy-start | bytes 24580
  1154.9 4.0 copy-start.28
  1154.9 5.6 copy-start.16
  1154.9 5.6 copy-start.30
  1157.2 6.1 copy-start.13
  1158.9 4.4 copy-start.52
  (22 other events, 46.6 us)
Sparse Core Ops, SparseCore 0:
  11.4 37.1 all-gather.4
  52.0 56.3 all-gather.6
  111.9 55.2 all-gather.8
  197.7 21.9 reduce-scatter.3
  308.6 71.4 all-reduce.14
  382.1 18.8 all-gather.10
  403.2 140.9 reduce-scatter.5
  546.5 136.8 reduce-scatter.7
  815.5 48.2 all-reduce.24
  883.1 51.9 all-reduce.22
  957.4 52.0 all-reduce.20
  1028.4 51.9 all-reduce.18
  1099.6 52.0 all-reduce.16
